TPU v7x, 128 devices: a whole 4x4x4 slice. The times are simulated.
128 devices in a mesh: box: 32 (over y, z, core), tx: 4 (over x).
Axes of the slice: x: 4, y: 4, z: 4, core: 2. Of those that a mesh axis runs over, the one named last changes fastest.
Arguments:
- bank: bfloat16 [512, 1024, 1024], P('box', 'tx'), may hold values from -6 to 6
- pick: int32 [64], replicated, may hold values from 0 to 1023, as said below
- slot_box: int32 [512], replicated, may hold values from 0 to 511, each once
- leaf_factor: bfloat16 [512, 512, 128], P('box'), may hold values from -0.1875 to 0.1875
- self_factor: bfloat16 [9, 512, 64, 128], P(None, 'box'), may hold values from -0.375 to 0.375
- cross_factor: bfloat16 [9, 512, 64, 128], P(None, 'box'), may hold values from -0.375 to 0.375
- target_factor: bfloat16 [512, 64, 4096], P('box'), may hold values from -0.5 to 0.5
Outputs:
- field: bfloat16 [512, 64, 4096], P('box', 'tx')
Inputs may be any that keep to these rules, and one draw needn't show every extreme that they name: `pick`: distinct stored transmitters. `slot_box`: each box once.
All inputs are finite; a program needn't handle non-finite values.
Results may differ from a plain program's by a relative error of at most 0.023.
Values may be sent and summed in bfloat16 or wider, within the bound.
A program may use at most 128 MiB of HBM per device.

v0:
```python
import jax
import jax.numpy as jnp
from jax import lax
from jax.sharding import PartitionSpec as P


def partner_2(block, axis, bit):
    count = lax.axis_size(axis)
    route = []
    for low in range(count):
        high = low | 1 << bit
        if high != low and high < count:
            route += [(low, high), (high, low)]
    return lax.ppermute(block, axis, route)


def complex_times(values, matrix):
    inner = matrix.shape[-2]
    half = matrix.shape[-1] // 2
    first = jnp.einsum(
        "brn,bnk->brk", values[..., :inner], matrix, preferred_element_type=jnp.float32
    )
    second = jnp.einsum(
        "brn,bnk->brk", values[..., inner:], matrix, preferred_element_type=jnp.float32
    )
    return jnp.concatenate(
        [first[..., :half] - second[..., half:], first[..., half:] + second[..., :half]], axis=-1
    )


def per_device(bank, pick, slot_box, leaf_factor, self_factor, cross_factor, target_factor):
    box_dev = bank.shape[0]
    bank_dev = bank.shape[1]
    tx_index = lax.axis_index("tx")
    local_pick = pick - tx_index * bank_dev
    chooser = (local_pick[:, None] == jnp.arange(bank_dev, dtype=jnp.int32)[None, :]).astype(
        jnp.bfloat16
    )
    picked = jnp.einsum("pj,bju->bpu", chooser, bank, preferred_element_type=jnp.float32)
    owned = lax.psum_scatter(picked.astype(jnp.bfloat16), "tx", scatter_dimension=1, tiled=True)
    coefs = complex_times(owned, leaf_factor).astype(jnp.bfloat16)
    box_index = lax.axis_index("box")
    sources = lax.dynamic_slice_in_dim(slot_box, box_index * box_dev, box_dev)
    piece = lax.all_gather(coefs, "box", axis=0, tiled=True)
    count = piece.shape[0]
    taker = (sources[:, None] == jnp.arange(count, dtype=jnp.int32)[None, :]).astype(jnp.bfloat16)
    current = jnp.einsum("sn,nrk->srk", taker, piece, preferred_element_type=jnp.float32).astype(
        jnp.bfloat16
    )
    levels = self_factor.shape[0]
    local_bits = box_dev.bit_length() - 1
    for level in range(levels):
        if level < local_bits:
            span = 1 << level
            shaped = current.reshape(
                box_dev // (2 * span), 2, span, current.shape[1], current.shape[2]
            )
            partner = jnp.flip(shaped, axis=1).reshape(current.shape)
        else:
            partner = partner_2(current, "box", level - local_bits)
        mixed = complex_times(current, self_factor[level]) + complex_times(
            partner, cross_factor[level]
        )
        current = mixed.astype(jnp.bfloat16)
    return complex_times(current, target_factor).astype(jnp.bfloat16)


def solution(mesh):
    in_specs = (
        P("box", "tx", None),
        P(),
        P(),
        P("box", None, None),
        P(None, "box", None, None),
        P(None, "box", None, None),
        P("box", None, None),
    )
    out_specs = P("box", "tx", None)
    return jax.shard_map(
        per_device, mesh=mesh, in_specs=in_specs, out_specs=out_specs, check_vma=False
    )
```

profile of v0, /device:TPU:0, one launch (start us, length us, event | category | flops | bytes accessed | tf_op | source)
XLA Modules:
  0.0 153.6 jit_solution(15288603705547300182)
XLA Ops:
  6.5 0.8 broadcast_subtract_fusion
  7.3 6.3 %convert_bitcast_fusion = bf16[16,64,1024]{2,1,0:T(8,128)(2,1)} fusion(bf16[16,256,1024]{2,1,0:T(8,128)(2,1)} %param.7, s32[64]{0:T(128)S(1)} %broadcast_subtract_fusion), kind=kOutput, calls=%fused_computation.7 | convolution fusion | flops 537935872 | bytes 10486016 | tf_op jit(solution)/shard_map/pj,bju->bpu/dot_general | solution.py:39
  13.8 32.2 %reduce-scatter.2.cloned.1.call-done = bf16[16,16,1024]{2,1,0:T(8,128)(2,1)} async-done(((bf16[16,64,1024]{2,1,0:T(8,128)(2,1)}), bf16[16,16,1024]{2,1,0:T(8,128)(2,1)}) %reduce-scatter.2.cloned.1.call-update) | async-done | bytes 524304 | tf_op jit(solution)/shard_map/reduce_scatter | solution.py:40
  46.0 1.4 fusion.7
  47.4 0.4 fusion.9
  47.9 0.7 pad_maximum_fusion.1
  48.7 0.8 dynamic_slice.3
  49.4 43.1 %all-gather.2.cloned.1.call-done = bf16[512,16,128]{2,1,0:T(8,128)(2,1)} async-done(((bf16[16,16,128]{2,1,0:T(8,128)(2,1)}), bf16[512,16,128]{2,1,0:T(8,128)(2,1)}) %all-gather.2.cloned.1.call-update) | async-done | bytes 2097168 | tf_op jit(solution)/shard_map/all_gather | solution.py:44
  92.6 2.0 %fusion.4 = bf16[16,16,128]{2,0,1:T(8,128)(2,1)S(1)} fusion(bf16[512,16,128]{2,1,0:T(8,128)(2,1)} %all-gather.2.cloned.1.call-done, s32[16]{0:T(128)S(1)} %dynamic_slice.3), kind=kOutput, calls=%fused_computation.8 | convolution fusion | flops 33595392 | bytes 2162752 | tf_op jit(solution)/shard_map/sn,nrk->srk/dot_general | solution.py:47
  94.6 0.3 rev.16
  94.9 1.2 fusion.75
  96.1 1.1 fusion.77
  97.4 1.1 fusion.81
  98.5 1.1 fusion.79
  100.1 1.2 fusion.67
  101.3 1.1 fusion.69
  102.5 1.2 fusion.71
  103.7 1.1 fusion.73
  105.4 1.2 fusion.59
  106.6 1.1 fusion.61
  107.7 1.2 fusion.63
  109.0 1.1 fusion.65
  110.7 1.3 fusion.51
  112.1 1.1 fusion.53
  113.2 1.4 fusion.55
  114.6 1.1 fusion.57
  116.1 0.3 collective-permute-start
  116.5 0.2 fusion.47
  117.0 0.4 collective-permute-done
  117.5 0.2 fusion.43
  118.2 1.3 collective-permute-start.1
  119.5 0.2 fusion.39
  120.0 2.5 %collective-permute-done.1 = bf16[16,16,128]{2,1,0:T(8,128)(2,1)S(1)} collective-permute-done((bf16[16,16,128]{2,1,0:T(8,128)(2,1)S(1)}, bf16[16,16,128]{2,1,0:T(8,128)(2,1)S(1)}, u32[]{:S(2)}, u32[]{:S(2)}) %collective-permute-start.1) | collective-permute-done | bytes 65568 | tf_op jit(solution)/shard_map/ppermute | solution.py:14
  122.5 0.2 fusion.35
  123.3 2.4 %collective-permute-start.2 = (bf16[16,16,128]{2,1,0:T(8,128)(2,1)S(1)}, bf16[16,16,128]{2,1,0:T(8,128)(2,1)S(1)}, u32[]{:S(2)}, u32[]{:S(2)}) collective-permute-start(bf16[16,16,128]{2,1,0:T(8,128)(2,1)S(1)} %fusion.129), channel_id=1, source_target_pairs={{0,16},{16,0},{4,20},{20,4},{8,24},{24,8},{12,28},{28,12},{32,48},... | collective-permute-start | bytes 196616 | tf_op jit(solution)/shard_map/ppermute | solution.py:14
  125.6 0.2 fusion.31
  126.2 2.9 %collective-permute-done.2 = bf16[16,16,128]{2,1,0:T(8,128)(2,1)S(1)} collective-permute-done((bf16[16,16,128]{2,1,0:T(8,128)(2,1)S(1)}, bf16[16,16,128]{2,1,0:T(8,128)(2,1)S(1)}, u32[]{:S(2)}, u32[]{:S(2)}) %collective-permute-start.2) | collective-permute-done | bytes 65568 | tf_op jit(solution)/shard_map/ppermute | solution.py:14
  129.1 0.2 fusion.27
  129.9 1.3 collective-permute-start.3
  131.7 2.5 %collective-permute-done.3 = bf16[16,16,128]{2,1,0:T(8,128)(2,1)S(1)} collective-permute-done((bf16[16,16,128]{2,1,0:T(8,128)(2,1)S(1)}, bf16[16,16,128]{2,1,0:T(8,128)(2,1)S(1)}, u32[]{:S(2)}, u32[]{:S(2)}) %collective-permute-start.3) | collective-permute-done | bytes 65568 | tf_op jit(solution)/shard_map/ppermute | solution.py:14
  134.2 0.2 fusion.19
  134.9 2.7 %collective-permute-start.4 = (bf16[16,16,128]{2,1,0:T(8,128)(2,1)S(1)}, bf16[16,16,128]{2,1,0:T(8,128)(2,1)S(1)}, u32[]{:S(2)}, u32[]{:S(2)}) collective-permute-start(bf16[16,16,128]{2,1,0:T(8,128)(2,1)S(1)} %fusion.131), channel_id=1, source_target_pairs={{0,64},{64,0},{4,68},{68,4},{8,72},{72,8},{12,76},{76,12},{16,80},... | collective-permute-start | bytes 196616 | tf_op jit(solution)/shard_map/ppermute | solution.py:14
  138.2 2.8 %collective-permute-done.4 = bf16[16,16,128]{2,1,0:T(8,128)(2,1)S(1)} collective-permute-done((bf16[16,16,128]{2,1,0:T(8,128)(2,1)S(1)}, bf16[16,16,128]{2,1,0:T(8,128)(2,1)S(1)}, u32[]{:S(2)}, u32[]{:S(2)}) %collective-permute-start.4) | collective-permute-done | bytes 65568 | tf_op jit(solution)/shard_map/ppermute | solution.py:14
  141.0 0.2 fusion.11
  141.7 1.3 fusion.133
  143.0 1.2 fusion.135
  144.2 1.1 fusion.1
  145.3 1.5 pad_maximum_fusion
  (64 shorter events, 6.9 us)
Async XLA Ops:
  6.5 39.4 %copy-start = (bf16[16,512,128]{2,1,0:T(8,128)(2,1)S(1)}, bf16[16,512,128]{2,1,0:T(8,128)(2,1)}, u32[]{:S(2)}) copy-start(bf16[16,512,128]{2,1,0:T(8,128)(2,1)} %param.10) | copy-start | bytes 6291460
  6.5 39.4 %reduce-scatter.2.cloned.1.call-start = ((), (), s32[]{:S(2)}) async-start(), calls=%async_computation.1 | async-start | bytes 2621440 | tf_op jit(solution)/shard_map/reduce_scatter | solution.py:40
  13.7 78.9 %all-gather.2.cloned.1.call-start = ((), (), s32[]{:S(2)}) async-start(), calls=%async_computation.2 | async-start | bytes 2162688 | tf_op jit(solution)/shard_map/all_gather | solution.py:44
  46.0 1.4 copy-start.3
  110.7 5.8 %copy-start.1 = (bf16[9,16,64,128]{3,2,1,0:T(8,128)(2,1)S(1)}, bf16[9,16,64,128]{3,2,1,0:T(8,128)(2,1)}, u32[]{:S(2)}) copy-start(bf16[9,16,64,128]{3,2,1,0:T(8,128)(2,1)} %param.11) | copy-start | bytes 7077892
  113.2 4.3 %copy-start.2 = (bf16[9,16,64,128]{3,2,1,0:T(8,128)(2,1)S(1)}, bf16[9,16,64,128]{3,2,1,0:T(8,128)(2,1)}, u32[]{:S(2)}) copy-start(bf16[9,16,64,128]{3,2,1,0:T(8,128)(2,1)} %param.12) | copy-start | bytes 7077892
  116.1 1.3 collective-permute-start
  118.2 4.3 %collective-permute-start.1 = (bf16[16,16,128]{2,1,0:T(8,128)(2,1)S(1)}, bf16[16,16,128]{2,1,0:T(8,128)(2,1)S(1)}, u32[]{:S(2)}, u32[]{:S(2)}) collective-permute-start(bf16[16,16,128]{2,1,0:T(8,128)(2,1)S(1)} %fusion.128), channel_id=1, source_target_pairs={{0,8},{8,0},{4,12},{12,4},{16,24},{24,16},{20,28},{28,20},{32,40},... | collective-permute-start | bytes 196616 | tf_op jit(solution)/shard_map/ppermute | solution.py:14
  119.9 21.8 %slice-start = ((s8[8388608]{0:T(1024)(128)(4,1)}), s8[4194304]{0:T(1024)(128)(4,1)S(1)}, s32[]{:S(2)}) async-start(s8[8388608]{0:T(1024)(128)(4,1)} %bitcast.120), calls=%async_computation.3 | async-start | bytes 8388608
  123.3 5.8 %collective-permute-start.2 = (bf16[16,16,128]{2,1,0:T(8,128)(2,1)S(1)}, bf16[16,16,128]{2,1,0:T(8,128)(2,1)S(1)}, u32[]{:S(2)}, u32[]{:S(2)}) collective-permute-start(bf16[16,16,128]{2,1,0:T(8,128)(2,1)S(1)} %fusion.129), channel_id=1, source_target_pairs={{0,16},{16,0},{4,20},{20,4},{8,24},{24,8},{12,28},{28,12},{32,48},... | collective-permute-start | bytes 196616 | tf_op jit(solution)/shard_map/ppermute | solution.py:14
  129.8 11.9 %slice-start.1 = ((s8[8388608]{0:T(1024)(128)(4,1)}), s8[4194304]{0:T(1024)(128)(4,1)S(1)}, s32[]{:S(2)}) async-start(s8[8388608]{0:T(1024)(128)(4,1)} %bitcast.120), calls=%async_computation.4 | async-start | bytes 8388608
  129.9 4.3 %collective-permute-start.3 = (bf16[16,16,128]{2,1,0:T(8,128)(2,1)S(1)}, bf16[16,16,128]{2,1,0:T(8,128)(2,1)S(1)}, u32[]{:S(2)}, u32[]{:S(2)}) collective-permute-start(bf16[16,16,128]{2,1,0:T(8,128)(2,1)S(1)} %fusion.130), channel_id=1, source_target_pairs={{0,32},{32,0},{4,36},{36,4},{8,40},{40,8},{12,44},{44,12},{16,48},... | collective-permute-start | bytes 196616 | tf_op jit(solution)/shard_map/ppermute | solution.py:14
  134.9 6.0 %collective-permute-start.4 = (bf16[16,16,128]{2,1,0:T(8,128)(2,1)S(1)}, bf16[16,16,128]{2,1,0:T(8,128)(2,1)S(1)}, u32[]{:S(2)}, u32[]{:S(2)}) collective-permute-start(bf16[16,16,128]{2,1,0:T(8,128)(2,1)S(1)} %fusion.131), channel_id=1, source_target_pairs={{0,64},{64,0},{4,68},{68,4},{8,72},{72,8},{12,76},{76,12},{16,80},... | collective-permute-start | bytes 196616 | tf_op jit(solution)/shard_map/ppermute | solution.py:14
Sparse Core Ops, SparseCore 0:
  13.8 32.0 reduce-scatter.1
  48.8 43.7 all-gather.1
where the time goes:
time: 154 us
  waiting for transfers between devices  86.4 us (56%)
  matrix products  35.8 us (23%)
  between operations  13.9 us (9%)
  other arithmetic  8.3 us (5%)
  starting transfers between devices  7.97 us (5%)
    all_gather x1, waiting for transfers between devices, per_device(): piece = lax.all_gather(coefs, 'box', axis=0, tiled=True)  43.1 us
    reduce_scatter x1, waiting for transfers between devices, per_device(): lax.psum_scatter(picked.astype(jnp.bfloat16), 'tx', scatter_dimension=1,...  32.2 us
    dot_general x20, matrix products, complex_times(): jnp.einsum('brn,bnk->brk', values[..., inner:], matrix, preferred_element...  15 us
    dot_general x20, matrix products, complex_times(): jnp.einsum('brn,bnk->brk', values[..., :inner], matrix, preferred_element...  12.5 us
    ppermute x5, waiting for transfers between devices, partner_2(): return lax.ppermute(block, axis, route)  11 us
    ppermute x5, starting transfers between devices, partner_2(): return lax.ppermute(block, axis, route)  7.93 us
    dot_general x1, matrix products, per_device(): jnp.einsum('pj,bju->bpu', chooser, bank, preferred_element_type=jnp.float32)  6.33 us
  transfers between devices with their start and end apart: 7, of which 7 were waited for; matrix products, arithmetic and copies ran while one was open for 2% of the time, Pallas kernels for 0%

commit v1 on v0

--- a/solution.py
+++ b/solution.py
@@ -2,6 +2,13 @@
 import jax.numpy as jnp
 from jax import lax
 from jax.sharding import PartitionSpec as P
+
+
+def _compute_inputs(array_here, link_axis):
+    later = lax.axis_size(link_axis)
+    y1 = jnp.stack([array_here] * later, axis=0)
+    h_now = lax.all_to_all(y1, link_axis, 0, 0)
+    return jnp.concatenate(h_now, axis=0)
 
 
 def partner_2(block, axis, bit):
@@ -41,7 +48,7 @@
     coefs = complex_times(owned, leaf_factor).astype(jnp.bfloat16)
     box_index = lax.axis_index("box")
     sources = lax.dynamic_slice_in_dim(slot_box, box_index * box_dev, box_dev)
-    piece = lax.all_gather(coefs, "box", axis=0, tiled=True)
+    piece = _compute_inputs(coefs, "box")
     count = piece.shape[0]
     taker = (sources[:, None] == jnp.arange(count, dtype=jnp.int32)[None, :]).astype(jnp.bfloat16)
     current = jnp.einsum("sn,nrk->srk", taker, piece, preferred_element_type=jnp.float32).astype(

time: 154 us -> 149 us (0.968)
  waiting for transfers between devices: 86.4 us -> 78.2 us
  local copies, waits for them, and re-layouts: 1.22 us -> 5.17 us
  matrix products: 35.8 us -> 34.2 us
    all_gather x1 -> x0, waiting for transfers between devices: 43.1 us -> none  [per_device(): piece = lax.all_gather(coefs, 'box', axis=0, tiled=True)]
    all_to_all x0 -> x1, waiting for transfers between devices: none -> 28.1 us  [_compute_inputs(): h_now = lax.all_to_all(y1, link_axis, 0, 0)]
    all_to_all x0 -> x1, starting transfers between devices: none -> 7.4 us  [_compute_inputs(): h_now = lax.all_to_all(y1, link_axis, 0, 0)]
    ppermute x5, waiting for transfers between devices: 11 us -> 17.8 us  [partner_2(): return lax.ppermute(block, axis, route)]
    ppermute x5, starting transfers between devices: 7.93 us -> 1.57 us  [partner_2(): return lax.ppermute(block, axis, route)]
    all_to_all x0 -> x1, local copies, waits for them, and re-layouts: none -> 2.13 us  [_compute_inputs(): h_now = lax.all_to_all(y1, link_axis, 0, 0)]
    another operation x0 -> x1, local copies, waits for them, and re-layouts: none -> 1.79 us  [_compute_inputs(): y1 = jnp.stack([array_here] * later, axis=0)]
    dot_general x1, matrix products: 2.02 us -> 0.42 us  [per_device(): jnp.einsum('sn,nrk->srk', taker, piece, preferred_element_type=jnp.float32)]
where the time goes in v1:
time: 149 us; the launch traced here: 148 us
  waiting for transfers between devices  78.2 us (52%)
  matrix products  34.2 us (23%)
  between operations  13.9 us (9%)
  starting transfers between devices  8.98 us (6%)
  other arithmetic  7.67 us (5%)
  local copies, waits for them, and re-layouts  5.17 us (3%)
    reduce_scatter x1, waiting for transfers between devices, per_device(): lax.psum_scatter(picked.astype(jnp.bfloat16), 'tx', scatter_dimension=1,...  32.2 us
    all_to_all x1, waiting for transfers between devices, _compute_inputs(): h_now = lax.all_to_all(y1, link_axis, 0, 0)  28.1 us
    ppermute x5, waiting for transfers between devices, partner_2(): return lax.ppermute(block, axis, route)  17.8 us
    dot_general x20, matrix products, complex_times(): jnp.einsum('brn,bnk->brk', values[..., inner:], matrix, preferred_element...  15 us
    dot_general x20, matrix products, complex_times(): jnp.einsum('brn,bnk->brk', values[..., :inner], matrix, preferred_element...  12.5 us
    all_to_all x1, starting transfers between devices, _compute_inputs(): h_now = lax.all_to_all(y1, link_axis, 0, 0)  7.4 us
    dot_general x1, matrix products, per_device(): jnp.einsum('pj,bju->bpu', chooser, bank, preferred_element_type=jnp.float32)  6.33 us
  transfers between devices with their start and end apart: 7, of which 7 were waited for; matrix products, arithmetic and copies ran while one was open for 2% of the time, Pallas kernels for 0%

profile of v1, /device:TPU:0, one launch (start us, length us, event | category | flops | bytes accessed | tf_op | source)
XLA Modules:
  0.0 148.1 jit_solution(6392007470722562417)
XLA Ops:
  6.5 0.8 broadcast_subtract_fusion
  7.3 6.3 %convert_bitcast_fusion = bf16[16,64,1024]{2,1,0:T(8,128)(2,1)} fusion(bf16[16,256,1024]{2,1,0:T(8,128)(2,1)} %param.7, s32[64]{0:T(128)S(1)} %broadcast_subtract_fusion), kind=kOutput, calls=%fused_computation.5 | convolution fusion | flops 537935872 | bytes 10486016 | tf_op jit(solution)/shard_map/pj,bju->bpu/dot_general | solution.py:46
  13.7 32.2 %reduce-scatter.2.cloned.1.call-done = bf16[16,16,1024]{2,1,0:T(8,128)(2,1)} async-done(((bf16[16,64,1024]{2,1,0:T(8,128)(2,1)}), bf16[16,16,1024]{2,1,0:T(8,128)(2,1)}) %reduce-scatter.2.cloned.1.call-update) | async-done | bytes 524304 | tf_op jit(solution)/shard_map/reduce_scatter | solution.py:47
  46.0 1.4 fusion.2
  47.4 0.4 fusion.4
  48.0 1.8 %stack.2 = bf16[32,16,16,128]{3,1,2,0:T(8,128)(2,1)} broadcast(bf16[16,16,128]{2,0,1:T(8,128)(2,1)S(1)} %copy.12), dimensions={1,2,3} | broadcast | bytes 2162688 | tf_op jit(solution)/shard_map/stack | solution.py:9
  49.8 7.4 %all-to-all-start = ((bf16[32,16,16,128]{3,1,2,0:T(8,128)(2,1)}), bf16[32,16,16,128]{3,1,2,0:T(8,128)(2,1)}, u32[]{:S(2)}, u32[]{:S(2)}) async-start(bf16[32,16,16,128]{3,1,2,0:T(8,128)(2,1)} %stack.2), calls=%async_computation.1 | async-start | bytes 4194304 | tf_op jit(solution)/shard_map/all_to_all | solution.py:10
  57.2 0.8 dynamic_slice.3
  58.0 28.1 %all-to-all-done = bf16[32,16,16,128]{3,1,2,0:T(8,128)(2,1)} async-done(((bf16[32,16,16,128]{3,1,2,0:T(8,128)(2,1)}), bf16[32,16,16,128]{3,1,2,0:T(8,128)(2,1)}, u32[]{:S(2)}, u32[]{:S(2)}) %all-to-all-start) | async-done | bytes 2097184 | tf_op jit(solution)/shard_map/all_to_all | solution.py:10
  86.1 2.1 %copy.13 = bf16[32,16,16,128]{3,1,0,2:T(8,128)(2,1)S(1)} copy(bf16[32,16,16,128]{3,1,2,0:T(8,128)(2,1)} %all-to-all-done) | data formatting | bytes 4194304 | tf_op jit(solution)/shard_map/all_to_all | solution.py:10
  88.3 0.4 convolution_convert_fusion
  88.7 0.3 rev.16
  89.0 1.2 fusion.70
  90.2 1.1 fusion.72
  91.5 1.1 fusion.76
  92.6 1.1 fusion.74
  94.3 1.2 fusion.62
  95.5 1.1 fusion.64
  96.6 1.2 fusion.66
  97.8 1.1 fusion.68
  99.5 1.2 fusion.54
  100.7 1.1 fusion.56
  101.9 1.2 fusion.58
  103.1 1.1 fusion.60
  104.8 1.3 fusion.46
  106.2 1.1 fusion.48
  107.3 1.4 fusion.50
  108.7 1.1 fusion.52
  110.3 0.2 fusion.42
  110.9 0.6 collective-permute-done
  111.6 0.2 fusion.38
  112.4 0.2 fusion.34
  113.0 3.7 %collective-permute-done.1 = bf16[16,16,128]{2,1,0:T(8,128)(2,1)S(1)} collective-permute-done((bf16[16,16,128]{2,1,0:T(8,128)(2,1)S(1)}, bf16[16,16,128]{2,1,0:T(8,128)(2,1)S(1)}, u32[]{:S(2)}, u32[]{:S(2)}) %collective-permute-start.1) | collective-permute-done | bytes 65568 | tf_op jit(solution)/shard_map/ppermute | solution.py:21
  116.7 0.2 fusion.30
  117.4 1.0 collective-permute-start.2
  119.0 4.3 %collective-permute-done.2 = bf16[16,16,128]{2,1,0:T(8,128)(2,1)S(1)} collective-permute-done((bf16[16,16,128]{2,1,0:T(8,128)(2,1)S(1)}, bf16[16,16,128]{2,1,0:T(8,128)(2,1)S(1)}, u32[]{:S(2)}, u32[]{:S(2)}) %collective-permute-start.2) | collective-permute-done | bytes 65568 | tf_op jit(solution)/shard_map/ppermute | solution.py:21
  123.2 0.2 fusion.22
  124.1 0.2 fusion.18
  124.7 4.1 %collective-permute-done.3 = bf16[16,16,128]{2,1,0:T(8,128)(2,1)S(1)} collective-permute-done((bf16[16,16,128]{2,1,0:T(8,128)(2,1)S(1)}, bf16[16,16,128]{2,1,0:T(8,128)(2,1)S(1)}, u32[]{:S(2)}, u32[]{:S(2)}) %collective-permute-start.3) | collective-permute-done | bytes 65568 | tf_op jit(solution)/shard_map/ppermute | solution.py:21
  128.7 0.2 fusion.14
  129.5 0.3 collective-permute-start.4
  129.8 0.2 fusion.10
  130.4 5.1 %collective-permute-done.4 = bf16[16,16,128]{2,1,0:T(8,128)(2,1)S(1)} collective-permute-done((bf16[16,16,128]{2,1,0:T(8,128)(2,1)S(1)}, bf16[16,16,128]{2,1,0:T(8,128)(2,1)S(1)}, u32[]{:S(2)}, u32[]{:S(2)}) %collective-permute-start.4) | collective-permute-done | bytes 65568 | tf_op jit(solution)/shard_map/ppermute | solution.py:21
  135.5 0.2 fusion.6
  136.3 1.3 fusion.128
  137.5 1.2 fusion.130
  138.8 1.1 fusion.1
  139.8 1.5 pad_maximum_fusion
  (66 shorter events, 7.0 us)
Async XLA Ops:
  6.5 39.4 %copy-start = (bf16[16,512,128]{2,1,0:T(8,128)(2,1)S(1)}, bf16[16,512,128]{2,1,0:T(8,128)(2,1)}, u32[]{:S(2)}) copy-start(bf16[16,512,128]{2,1,0:T(8,128)(2,1)} %param.10) | copy-start | bytes 6291460
  6.5 39.4 %reduce-scatter.2.cloned.1.call-start = ((), (), s32[]{:S(2)}) async-start(), calls=%async_computation.2 | async-start | bytes 2621440 | tf_op jit(solution)/shard_map/reduce_scatter | solution.py:47
  46.0 1.4 copy-start.3
  49.8 36.3 %all-to-all-start = ((bf16[32,16,16,128]{3,1,2,0:T(8,128)(2,1)}), bf16[32,16,16,128]{3,1,2,0:T(8,128)(2,1)}, u32[]{:S(2)}, u32[]{:S(2)}) async-start(bf16[32,16,16,128]{3,1,2,0:T(8,128)(2,1)} %stack.2), calls=%async_computation.1 | async-start | bytes 4194304 | tf_op jit(solution)/shard_map/all_to_all | solution.py:10
  104.8 5.5 %copy-start.1 = (bf16[9,16,64,128]{3,2,1,0:T(8,128)(2,1)S(1)}, bf16[9,16,64,128]{3,2,1,0:T(8,128)(2,1)}, u32[]{:S(2)}) copy-start(bf16[9,16,64,128]{3,2,1,0:T(8,128)(2,1)} %param.11) | copy-start | bytes 7077892
  107.3 4.3 %copy-start.2 = (bf16[9,16,64,128]{3,2,1,0:T(8,128)(2,1)S(1)}, bf16[9,16,64,128]{3,2,1,0:T(8,128)(2,1)}, u32[]{:S(2)}) copy-start(bf16[9,16,64,128]{3,2,1,0:T(8,128)(2,1)} %param.12) | copy-start | bytes 7077892
  110.2 1.3 collective-permute-start
  112.3 4.3 %collective-permute-start.1 = (bf16[16,16,128]{2,1,0:T(8,128)(2,1)S(1)}, bf16[16,16,128]{2,1,0:T(8,128)(2,1)S(1)}, u32[]{:S(2)}, u32[]{:S(2)}) collective-permute-start(bf16[16,16,128]{2,1,0:T(8,128)(2,1)S(1)} %fusion.123), channel_id=1, source_target_pairs={{0,8},{8,0},{4,12},{12,4},{16,24},{24,16},{20,28},{28,20},{32,40},... | collective-permute-start | bytes 196616 | tf_op jit(solution)/shard_map/ppermute | solution.py:21
  112.8 23.4 %slice-start = ((s8[8388608]{0:T(1024)(128)(4,1)}), s8[4194304]{0:T(1024)(128)(4,1)S(1)}, s32[]{:S(2)}) async-start(s8[8388608]{0:T(1024)(128)(4,1)} %bitcast.122), calls=%async_computation.3 | async-start | bytes 8388608
  117.4 5.8 %collective-permute-start.2 = (bf16[16,16,128]{2,1,0:T(8,128)(2,1)S(1)}, bf16[16,16,128]{2,1,0:T(8,128)(2,1)S(1)}, u32[]{:S(2)}, u32[]{:S(2)}) collective-permute-start(bf16[16,16,128]{2,1,0:T(8,128)(2,1)S(1)} %fusion.124), channel_id=1, source_target_pairs={{0,16},{16,0},{4,20},{20,4},{8,24},{24,8},{12,28},{28,12},{32,48},... | collective-permute-start | bytes 196616 | tf_op jit(solution)/shard_map/ppermute | solution.py:21
  124.0 12.3 %slice-start.1 = ((s8[8388608]{0:T(1024)(128)(4,1)}), s8[4194304]{0:T(1024)(128)(4,1)S(1)}, s32[]{:S(2)}) async-start(s8[8388608]{0:T(1024)(128)(4,1)} %bitcast.122), calls=%async_computation.4 | async-start | bytes 8388608
  124.0 4.8 %collective-permute-start.3 = (bf16[16,16,128]{2,1,0:T(8,128)(2,1)S(1)}, bf16[16,16,128]{2,1,0:T(8,128)(2,1)S(1)}, u32[]{:S(2)}, u32[]{:S(2)}) collective-permute-start(bf16[16,16,128]{2,1,0:T(8,128)(2,1)S(1)} %fusion.125), channel_id=1, source_target_pairs={{0,32},{32,0},{4,36},{36,4},{8,40},{40,8},{12,44},{44,12},{16,48},... | collective-permute-start | bytes 196616 | tf_op jit(solution)/shard_map/ppermute | solution.py:21
  129.5 6.0 %collective-permute-start.4 = (bf16[16,16,128]{2,1,0:T(8,128)(2,1)S(1)}, bf16[16,16,128]{2,1,0:T(8,128)(2,1)S(1)}, u32[]{:S(2)}, u32[]{:S(2)}) collective-permute-start(bf16[16,16,128]{2,1,0:T(8,128)(2,1)S(1)} %fusion.126), channel_id=1, source_target_pairs={{0,64},{64,0},{4,68},{68,4},{8,72},{72,8},{12,76},{76,12},{16,80},... | collective-permute-start | bytes 196616 | tf_op jit(solution)/shard_map/ppermute | solution.py:21
Sparse Core Ops, SparseCore 0:
  13.8 32.0 reduce-scatter.1
